TPU v7x, 128 devices: a whole 4x4x4 slice. The times are simulated.
128 devices in a mesh: smp: 8 (over x_lo, z), bld: 16 (over y, x_hi, core).
Axes of the slice: x: 4 (x_hi: 2, x_lo: 2; x = x_hi * 2 + x_lo), y: 4, z: 4, core: 2. Of those that a mesh axis runs over, the one named last changes fastest.
Arguments:
- tensor: bfloat16 [4, 8192, 16384], P(None, 'smp', 'bld'), may hold values from -576 to 576
- building_factor: float32 [64, 16384], P(None, 'bld'), may hold values from -144 to 144
- hour_weights: float32 [4, 64], replicated, may hold values from -5 to 5
Outputs:
- sample_factor: float32 [64, 8192], P(None, ('smp', 'bld'))
- building_out: float32 [64, 16384], P(None, ('bld', 'smp'))
- hour_out: float32 [4, 64], replicated
All inputs are finite; a program needn't handle non-finite values.
Results may differ from a plain program's by a relative error of at most 0.008.
Values may be sent and summed in bfloat16 or wider, within the bound.
A program may use at most 64 MiB of HBM per device.

v0:
```python
import math
import jax
import jax.numpy as jnp
from jax import lax
from jax.sharding import PartitionSpec as P

SWEEPS = 5
EPSILON = 1e-06
RIDGE_SHARE = 0.05


def regularized(gram):
    order_size = gram.shape[0]
    return gram + RIDGE_SHARE * jnp.mean(jnp.diagonal(gram)) * jnp.eye(order_size, dtype=gram.dtype)


def solve_rows(gram, right_side):
    lower_factor = jnp.linalg.cholesky(regularized(gram))
    middle = lax.linalg.triangular_solve(lower_factor, right_side, left_side=True, lower=True)
    return lax.linalg.triangular_solve(
        lower_factor, middle, left_side=True, lower=True, transpose_a=True
    )


def finish(unscaled, gram_raw, row_count):
    column_norm = jnp.sqrt(jnp.diagonal(gram_raw) / row_count + EPSILON)
    return (
        unscaled / column_norm[:, None],
        gram_raw / (column_norm[:, None] * column_norm[None, :]),
    )


def hour_gram(hourly):
    return jnp.dot(hourly.T, hourly, precision=lax.Precision.HIGHEST)


def self_gram(unscaled):
    return jnp.dot(unscaled, unscaled.T, precision=lax.Precision.HIGHEST)


def local(tensor, building_factor, hour_weights):
    samples_total = tensor.shape[1] * lax.axis_size("smp")
    buildings_total = tensor.shape[2] * lax.axis_size("bld")
    scale_up = math.sqrt(samples_total * buildings_total)
    hourly = hour_weights / scale_up
    gram_build = lax.psum(self_gram(building_factor), "bld")
    build_low = building_factor.astype(jnp.bfloat16)
    partial_value = jnp.einsum("rj,kij->kri", build_low, tensor, preferred_element_type=jnp.float32)
    sample_out = None
    building_out = None
    for sweep_index in range(SWEEPS):
        sample_terms = jnp.sum(hourly[:, :, None] * partial_value, axis=0)
        sample_rhs = lax.psum(sample_terms, "bld")
        unscaled = solve_rows(gram_build * hour_gram(hourly), sample_rhs)
        gram_raw = lax.psum(self_gram(unscaled), "smp")
        samples_now, gram_sample = finish(unscaled, gram_raw, samples_total)
        sample_low = samples_now.astype(jnp.bfloat16)
        share_width = samples_now.shape[1] // lax.axis_size("bld")
        sample_out = lax.dynamic_slice_in_dim(
            samples_now, lax.axis_index("bld") * share_width, share_width, 1
        )
        mixed = jnp.einsum("ri,kij->krj", sample_low, tensor, preferred_element_type=jnp.float32)
        build_terms = jnp.sum(hourly[:, :, None] * mixed, axis=0)
        build_rhs = lax.psum(build_terms, "smp")
        unscaled = solve_rows(gram_sample * hour_gram(hourly), build_rhs)
        gram_raw = lax.psum(self_gram(unscaled), "bld")
        building_now, gram_build = finish(unscaled, gram_raw, buildings_total)
        build_low = building_now.astype(jnp.bfloat16)
        share_width = building_now.shape[1] // lax.axis_size("smp")
        building_out = lax.dynamic_slice_in_dim(
            building_now, lax.axis_index("smp") * share_width, share_width, 1
        )
        partial_value = jnp.einsum(
            "rj,kij->kri", build_low, tensor, preferred_element_type=jnp.float32
        )
        hour_terms = jnp.sum(sample_low.astype(jnp.float32)[None, :, :] * partial_value, axis=2)
        hour_rhs = lax.psum(hour_terms, ("smp", "bld"))
        hourly = solve_rows(gram_sample * gram_build, hour_rhs.T).T
    return (sample_out, building_out, hourly * scale_up)


def solution(mesh):
    in_specs = (P(None, "smp", "bld"), P(None, "bld"), P())
    out_specs = (P(None, ("smp", "bld")), P(None, ("bld", "smp")), P())
    return jax.shard_map(local, mesh=mesh, in_specs=in_specs, out_specs=out_specs, check_vma=False)
```

profile of v0, /device:TPU:1, one launch (start us, length us, event | category | flops | bytes accessed | tf_op | source)
XLA Modules:
  0.0 2094.5 jit_solution(17855161390660669668)
XLA Ops:
  15.2 65.3 %psum.182 = f32[64,64]{0,1:T(8,128)S(1)} all-reduce(f32[64,64]{0,1:T(8,128)S(1)} %fusion.159), channel_id=1, replica_groups=mesh['smp'=8,'bld'=16] {'bld'}, use_global_device_ids=true, to_apply=%region_0.0 | all-reduce | flops 4096 | bytes 32768 | tf_op jit(solution)/shard_map/psum | solution.py:46
  95.0 60.6 %all-reduce.11.cloned.1.call-done = f32[64,1024]{1,0:T(8,128)} async-done(((f32[64,1024]{1,0:T(8,128)}), f32[64,1024]{1,0:T(8,128)}) %all-reduce.11.cloned.1.call-update) | async-done | bytes 262160 | tf_op jit(solution)/shard_map/psum | solution.py:53
  157.7 26.2 %psum.184 = f32[64,64]{0,1:T(8,128)S(1)} all-reduce(f32[64,64]{0,1:T(8,128)S(1)} %fusion.160), channel_id=1, replica_groups=mesh['smp'=8,'bld'=16] {'smp'}, use_global_device_ids=true, to_apply=%region_6.10 | all-reduce | flops 4096 | bytes 32768 | tf_op jit(solution)/shard_map/psum | solution.py:55
  205.1 65.8 %all-reduce.13.cloned.1.call-done = f32[64,1024]{1,0:T(8,128)} async-done(((f32[64,1024]{1,0:T(8,128)}), f32[64,1024]{1,0:T(8,128)}) %all-reduce.13.cloned.1.call-update) | async-done | bytes 262160 | tf_op jit(solution)/shard_map/psum | solution.py:64
  273.0 65.3 %psum.186 = f32[64,64]{0,1:T(8,128)S(1)} all-reduce(f32[64,64]{0,1:T(8,128)S(1)} %fusion.161), channel_id=1, replica_groups=mesh['smp'=8,'bld'=16] {'bld'}, use_global_device_ids=true, to_apply=%region_10.14 | all-reduce | flops 4096 | bytes 32768 | tf_op jit(solution)/shard_map/psum | solution.py:66
  359.6 67.3 %psum.187 = f32[64,4]{0,1:T(4,128)S(1)} all-reduce(f32[64,4]{0,1:T(4,128)S(1)} %bitcast.367), channel_id=1, replica_groups=mesh['smp'=8,'bld'=16] {'smp','bld'}, use_global_device_ids=true, to_apply=%region_13.17 | all-reduce | flops 256 | bytes 2048 | tf_op jit(solution)/shard_map/psum | solution.py:77
  442.7 127.8 %all-reduce.15.cloned.1.call-done = f32[64,1024]{1,0:T(8,128)} async-done(((f32[64,1024]{1,0:T(8,128)}), f32[64,1024]{1,0:T(8,128)}) %all-reduce.15.cloned.1.call-update) | async-done | bytes 262160 | tf_op jit(solution)/shard_map/psum | solution.py:53
  572.6 26.5 %psum.189 = f32[64,64]{0,1:T(8,128)S(1)} all-reduce(f32[64,64]{0,1:T(8,128)S(1)} %fusion.162), channel_id=1, replica_groups=mesh['smp'=8,'bld'=16] {'smp'}, use_global_device_ids=true, to_apply=%region_17.23 | all-reduce | flops 4096 | bytes 32768 | tf_op jit(solution)/shard_map/psum | solution.py:55
  620.2 65.8 %all-reduce.17.cloned.1.call-done = f32[64,1024]{1,0:T(8,128)} async-done(((f32[64,1024]{1,0:T(8,128)}), f32[64,1024]{1,0:T(8,128)}) %all-reduce.17.cloned.1.call-update) | async-done | bytes 262160 | tf_op jit(solution)/shard_map/psum | solution.py:64
  688.1 64.7 %psum.191 = f32[64,64]{0,1:T(8,128)S(1)} all-reduce(f32[64,64]{0,1:T(8,128)S(1)} %fusion.163), channel_id=1, replica_groups=mesh['smp'=8,'bld'=16] {'bld'}, use_global_device_ids=true, to_apply=%region_21.27 | all-reduce | flops 4096 | bytes 32768 | tf_op jit(solution)/shard_map/psum | solution.py:66
  774.2 67.5 %psum.192 = f32[64,4]{0,1:T(4,128)S(1)} all-reduce(f32[64,4]{0,1:T(4,128)S(1)} %bitcast.368), channel_id=1, replica_groups=mesh['smp'=8,'bld'=16] {'smp','bld'}, use_global_device_ids=true, to_apply=%region_24.30 | all-reduce | flops 256 | bytes 2048 | tf_op jit(solution)/shard_map/psum | solution.py:77
  857.5 127.8 %all-reduce.19.cloned.1.call-done = f32[64,1024]{1,0:T(8,128)} async-done(((f32[64,1024]{1,0:T(8,128)}), f32[64,1024]{1,0:T(8,128)}) %all-reduce.19.cloned.1.call-update) | async-done | bytes 262160 | tf_op jit(solution)/shard_map/psum | solution.py:53
  1034.7 65.8 %all-reduce.21.cloned.1.call-done = f32[64,1024]{1,0:T(8,128)} async-done(((f32[64,1024]{1,0:T(8,128)}), f32[64,1024]{1,0:T(8,128)}) %all-reduce.21.cloned.1.call-update) | async-done | bytes 262160 | tf_op jit(solution)/shard_map/psum | solution.py:64
  1102.6 65.2 %psum.196 = f32[64,64]{0,1:T(8,128)S(1)} all-reduce(f32[64,64]{0,1:T(8,128)S(1)} %fusion.165), channel_id=1, replica_groups=mesh['smp'=8,'bld'=16] {'bld'}, use_global_device_ids=true, to_apply=%region_32.38 | all-reduce | flops 4096 | bytes 32768 | tf_op jit(solution)/shard_map/psum | solution.py:66
  1189.1 67.3 %psum.197 = f32[64,4]{0,1:T(4,128)S(1)} all-reduce(f32[64,4]{0,1:T(4,128)S(1)} %bitcast.369), channel_id=1, replica_groups=mesh['smp'=8,'bld'=16] {'smp','bld'}, use_global_device_ids=true, to_apply=%region_35.41 | all-reduce | flops 256 | bytes 2048 | tf_op jit(solution)/shard_map/psum | solution.py:77
  1272.2 127.8 %all-reduce.23.cloned.1.call-done = f32[64,1024]{1,0:T(8,128)} async-done(((f32[64,1024]{1,0:T(8,128)}), f32[64,1024]{1,0:T(8,128)}) %all-reduce.23.cloned.1.call-update) | async-done | bytes 262160 | tf_op jit(solution)/shard_map/psum | solution.py:53
  1402.0 26.5 %psum.199 = f32[64,64]{0,1:T(8,128)S(1)} all-reduce(f32[64,64]{0,1:T(8,128)S(1)} %fusion.166), channel_id=1, replica_groups=mesh['smp'=8,'bld'=16] {'smp'}, use_global_device_ids=true, to_apply=%region_39.45 | all-reduce | flops 4096 | bytes 32768 | tf_op jit(solution)/shard_map/psum | solution.py:55
  1449.7 65.8 %all-reduce.25.cloned.1.call-done = f32[64,1024]{1,0:T(8,128)} async-done(((f32[64,1024]{1,0:T(8,128)}), f32[64,1024]{1,0:T(8,128)}) %all-reduce.25.cloned.1.call-update) | async-done | bytes 262160 | tf_op jit(solution)/shard_map/psum | solution.py:64
  1517.6 64.7 %psum.201 = f32[64,64]{0,1:T(8,128)S(1)} all-reduce(f32[64,64]{0,1:T(8,128)S(1)} %fusion.167), channel_id=1, replica_groups=mesh['smp'=8,'bld'=16] {'bld'}, use_global_device_ids=true, to_apply=%region_43.49 | all-reduce | flops 4096 | bytes 32768 | tf_op jit(solution)/shard_map/psum | solution.py:66
  1603.6 67.5 %psum.202 = f32[64,4]{0,1:T(4,128)S(1)} all-reduce(f32[64,4]{0,1:T(4,128)S(1)} %bitcast.370), channel_id=1, replica_groups=mesh['smp'=8,'bld'=16] {'smp','bld'}, use_global_device_ids=true, to_apply=%region_46.52 | all-reduce | flops 256 | bytes 2048 | tf_op jit(solution)/shard_map/psum | solution.py:77
  1686.9 127.8 %all-reduce.27.cloned.1.call-done = f32[64,1024]{1,0:T(8,128)} async-done(((f32[64,1024]{1,0:T(8,128)}), f32[64,1024]{1,0:T(8,128)}) %all-reduce.27.cloned.1.call-update) | async-done | bytes 262160 | tf_op jit(solution)/shard_map/psum | solution.py:53
  1864.7 65.3 %all-reduce.29.cloned.1.call-done = f32[64,1024]{1,0:T(8,128)} async-done(((f32[64,1024]{1,0:T(8,128)}), f32[64,1024]{1,0:T(8,128)}) %all-reduce.29.cloned.1.call-update) | async-done | bytes 262160 | tf_op jit(solution)/shard_map/psum | solution.py:64
  1932.1 65.0 %psum.206 = f32[64,64]{0,1:T(8,128)S(1)} all-reduce(f32[64,64]{0,1:T(8,128)S(1)} %fusion.169), channel_id=1, replica_groups=mesh['smp'=8,'bld'=16] {'bld'}, use_global_device_ids=true, to_apply=%region_54.60 | all-reduce | flops 4096 | bytes 32768 | tf_op jit(solution)/shard_map/psum | solution.py:66
  2018.5 67.3 %psum.207 = f32[64,4]{0,1:T(4,128)S(1)} all-reduce(f32[64,4]{0,1:T(4,128)S(1)} %fusion.11), channel_id=1, replica_groups=mesh['smp'=8,'bld'=16] {'smp','bld'}, use_global_device_ids=true, to_apply=%region_57.63 | all-reduce | flops 256 | bytes 2048 | tf_op jit(solution)/shard_map/psum | solution.py:77
  (277 shorter events, 362.7 us)
Async XLA Ops:
  7.2 73.3 %copy-start.1 = (f32[4,64]{1,0:T(4,128)S(1)}, f32[4,64]{1,0:T(4,128)}, u32[]{:S(2)}) copy-start(f32[4,64]{1,0:T(4,128)} %param.14) | copy-start | bytes 3076
  7.2 7.6 copy-start
  7.2 148.4 %all-reduce.11.cloned.1.call-start = ((), (), s32[]{:S(2)}) async-start(), calls=%async_computation | async-start | bytes 524288 | tf_op jit(solution)/shard_map/psum | solution.py:53
  14.7 256.2 %all-reduce.13.cloned.1.call-start = ((), (), s32[]{:S(2)}) async-start(), calls=%async_computation.1 | async-start | bytes 524288 | tf_op jit(solution)/shard_map/psum | solution.py:64
  199.4 371.1 %all-reduce.15.cloned.1.call-start = ((), (), s32[]{:S(2)}) async-start(), calls=%async_computation.2 | async-start | bytes 524288 | tf_op jit(solution)/shard_map/psum | solution.py:53
  436.5 249.5 %all-reduce.17.cloned.1.call-start = ((), (), s32[]{:S(2)}) async-start(), calls=%async_computation.3 | async-start | bytes 524288 | tf_op jit(solution)/shard_map/psum | solution.py:64
  614.5 370.8 %all-reduce.19.cloned.1.call-start = ((), (), s32[]{:S(2)}) async-start(), calls=%async_computation.4 | async-start | bytes 524288 | tf_op jit(solution)/shard_map/psum | solution.py:53
  851.2 249.2 %all-reduce.21.cloned.1.call-start = ((), (), s32[]{:S(2)}) async-start(), calls=%async_computation.5 | async-start | bytes 524288 | tf_op jit(solution)/shard_map/psum | solution.py:64
  1029.0 371.0 %all-reduce.23.cloned.1.call-start = ((), (), s32[]{:S(2)}) async-start(), calls=%async_computation.6 | async-start | bytes 524288 | tf_op jit(solution)/shard_map/psum | solution.py:53
  1265.9 249.5 %all-reduce.25.cloned.1.call-start = ((), (), s32[]{:S(2)}) async-start(), calls=%async_computation.7 | async-start | bytes 524288 | tf_op jit(solution)/shard_map/psum | solution.py:64
  1443.9 370.8 %all-reduce.27.cloned.1.call-start = ((), (), s32[]{:S(2)}) async-start(), calls=%async_computation.8 | async-start | bytes 524288 | tf_op jit(solution)/shard_map/psum | solution.py:53
  1680.7 249.3 %all-reduce.29.cloned.1.call-start = ((), (), s32[]{:S(2)}) async-start(), calls=%async_computation.9 | async-start | bytes 524288 | tf_op jit(solution)/shard_map/psum | solution.py:64
Sparse Core Ops, SparseCore 0:
  14.8 140.7 all-reduce.10
  199.5 71.3 all-reduce.12
  436.6 133.8 all-reduce.14
  614.6 71.3 all-reduce.16
  851.4 133.8 all-reduce.18
  1029.1 71.3 all-reduce.20
  1266.0 133.8 all-reduce.22
  1444.1 71.3 all-reduce.24
  1680.8 133.8 all-reduce.26
  1858.6 71.3 all-reduce.28
where the time goes:
time: 2100 us; the launch traced here: 2090 us
  waiting for transfers between devices  900 us (43%)
  blocking collectives  859 us (41%)
  other arithmetic  196 us (9%)
  matrix products  90.9 us (4%)
  between operations  25.1 us (1%)
  local copies, waits for them, and re-layouts  22.6 us (1%)
    psum x5, waiting for transfers between devices, local(): sample_rhs = lax.psum(sample_terms, 'bld')  572 us
    psum x5, blocking collectives, local(): hour_rhs = lax.psum(hour_terms, ('smp', 'bld'))  337 us
    psum x5, waiting for transfers between devices, local(): build_rhs = lax.psum(build_terms, 'smp')  328 us
    psum x5, blocking collectives, local(): gram_raw = lax.psum(self_gram(unscaled), 'bld')  325 us
    psum x5, blocking collectives, local(): gram_raw = lax.psum(self_gram(unscaled), 'smp')  132 us
    another operation x45, other arithmetic, solve_rows(): lower_factor = jnp.linalg.cholesky(regularized(gram))  97.7 us
    another operation x30, other arithmetic, solve_rows(): lax.linalg.triangular_solve(lower_factor, middle, left_side=True, lower=T...  83.3 us
    psum x1, blocking collectives, local(): gram_build = lax.psum(self_gram(building_factor), 'bld')  65.3 us
  transfers between devices with their start and end apart: 10, of which 10 were waited for; matrix products, arithmetic and copies ran while one was open for 3% of the time, Pallas kernels for 0%

commit v1 on v0

--- a/solution.py
+++ b/solution.py
@@ -74,7 +74,7 @@
             "rj,kij->kri", build_low, tensor, preferred_element_type=jnp.float32
         )
         hour_terms = jnp.sum(sample_low.astype(jnp.float32)[None, :, :] * partial_value, axis=2)
-        hour_rhs = lax.psum(hour_terms, ("smp", "bld"))
+        hour_rhs = lax.psum(lax.psum(hour_terms, "smp"), "bld")
         hourly = solve_rows(gram_sample * gram_build, hour_rhs.T).T
     return (sample_out, building_out, hourly * scale_up)
 

time: 2100 us -> 2030 us (0.967)
  blocking collectives: 859 us -> 801 us
    psum x5 -> x10, blocking collectives: 337 us -> 279 us  [local(): hour_rhs = lax.psum(lax.psum(hour_terms, 'smp'), 'bld')]
where the time goes in v1:
time: 2030 us
  waiting for transfers between devices  888 us (44%)
  blocking collectives  801 us (39%)
  other arithmetic  196 us (10%)
  matrix products  90.9 us (4%)
  between operations  25.4 us (1%)
  local copies, waits for them, and re-layouts  22.6 us (1%)
    psum x5, waiting for transfers between devices, local(): sample_rhs = lax.psum(sample_terms, 'bld')  561 us
    psum x5, waiting for transfers between devices, local(): build_rhs = lax.psum(build_terms, 'smp')  327 us
    psum x5, blocking collectives, local(): gram_raw = lax.psum(self_gram(unscaled), 'bld')  324 us
    psum x10, blocking collectives, local(): hour_rhs = lax.psum(lax.psum(hour_terms, 'smp'), 'bld')  279 us
    psum x5, blocking collectives, local(): gram_raw = lax.psum(self_gram(unscaled), 'smp')  132 us
    another operation x45, other arithmetic, solve_rows(): lower_factor = jnp.linalg.cholesky(regularized(gram))  97.7 us
    another operation x30, other arithmetic, solve_rows(): lax.linalg.triangular_solve(lower_factor, middle, left_side=True, lower=T...  83.3 us
    psum x1, blocking collectives, local(): gram_build = lax.psum(self_gram(building_factor), 'bld')  65.3 us
  transfers between devices with their start and end apart: 10, of which 10 were waited for; matrix products, arithmetic and copies ran while one was open for 3% of the time, Pallas kernels for 0%

profile of v1, /device:TPU:1, one launch (start us, length us, event | category | flops | bytes accessed | tf_op | source)
XLA Modules:
  0.0 2025.4 jit_solution(12484149870965406778)
XLA Ops:
  15.2 65.3 %psum.217 = f32[64,64]{0,1:T(8,128)S(1)} all-reduce(f32[64,64]{0,1:T(8,128)S(1)} %fusion.159), channel_id=1, replica_groups=mesh['smp'=8,'bld'=16] {'bld'}, use_global_device_ids=true, to_apply=%region_0.0 | all-reduce | flops 4096 | bytes 32768 | tf_op jit(solution)/shard_map/psum | solution.py:46
  95.0 60.6 %all-reduce.11.cloned.1.call-done = f32[64,1024]{1,0:T(8,128)} async-done(((f32[64,1024]{1,0:T(8,128)}), f32[64,1024]{1,0:T(8,128)}) %all-reduce.11.cloned.1.call-update) | async-done | bytes 262160 | tf_op jit(solution)/shard_map/psum | solution.py:53
  157.7 26.2 %psum.219 = f32[64,64]{0,1:T(8,128)S(1)} all-reduce(f32[64,64]{0,1:T(8,128)S(1)} %fusion.160), channel_id=1, replica_groups=mesh['smp'=8,'bld'=16] {'smp'}, use_global_device_ids=true, to_apply=%region_6.10 | all-reduce | flops 4096 | bytes 32768 | tf_op jit(solution)/shard_map/psum | solution.py:55
  205.1 65.8 %all-reduce.13.cloned.1.call-done = f32[64,1024]{1,0:T(8,128)} async-done(((f32[64,1024]{1,0:T(8,128)}), f32[64,1024]{1,0:T(8,128)}) %all-reduce.13.cloned.1.call-update) | async-done | bytes 262160 | tf_op jit(solution)/shard_map/psum | solution.py:64
  273.0 65.0 %psum.221 = f32[64,64]{0,1:T(8,128)S(1)} all-reduce(f32[64,64]{0,1:T(8,128)S(1)} %fusion.161), channel_id=1, replica_groups=mesh['smp'=8,'bld'=16] {'bld'}, use_global_device_ids=true, to_apply=%region_10.14 | all-reduce | flops 4096 | bytes 32768 | tf_op jit(solution)/shard_map/psum | solution.py:66
  373.0 42.1 %psum.223 = f32[64,4]{0,1:T(4,128)S(1)} all-reduce(f32[64,4]{0,1:T(4,128)S(1)} %bitcast.370), channel_id=1, replica_groups=mesh['smp'=8,'bld'=16] {'bld'}, use_global_device_ids=true, to_apply=%region_14.18 | all-reduce | flops 256 | bytes 2048 | tf_op jit(solution)/shard_map/psum | solution.py:77
  430.9 125.2 %all-reduce.15.cloned.1.call-done = f32[64,1024]{1,0:T(8,128)} async-done(((f32[64,1024]{1,0:T(8,128)}), f32[64,1024]{1,0:T(8,128)}) %all-reduce.15.cloned.1.call-update) | async-done | bytes 262160 | tf_op jit(solution)/shard_map/psum | solution.py:53
  558.2 26.5 %psum.225 = f32[64,64]{0,1:T(8,128)S(1)} all-reduce(f32[64,64]{0,1:T(8,128)S(1)} %fusion.162), channel_id=1, replica_groups=mesh['smp'=8,'bld'=16] {'smp'}, use_global_device_ids=true, to_apply=%region_18.24 | all-reduce | flops 4096 | bytes 32768 | tf_op jit(solution)/shard_map/psum | solution.py:55
  606.3 65.0 %all-reduce.17.cloned.1.call-done = f32[64,1024]{1,0:T(8,128)} async-done(((f32[64,1024]{1,0:T(8,128)}), f32[64,1024]{1,0:T(8,128)}) %all-reduce.17.cloned.1.call-update) | async-done | bytes 262160 | tf_op jit(solution)/shard_map/psum | solution.py:64
  673.4 64.7 %psum.227 = f32[64,64]{0,1:T(8,128)S(1)} all-reduce(f32[64,64]{0,1:T(8,128)S(1)} %fusion.163), channel_id=1, replica_groups=mesh['smp'=8,'bld'=16] {'bld'}, use_global_device_ids=true, to_apply=%region_22.28 | all-reduce | flops 4096 | bytes 32768 | tf_op jit(solution)/shard_map/psum | solution.py:66
  773.2 42.1 %psum.229 = f32[64,4]{0,1:T(4,128)S(1)} all-reduce(f32[64,4]{0,1:T(4,128)S(1)} %bitcast.371), channel_id=1, replica_groups=mesh['smp'=8,'bld'=16] {'bld'}, use_global_device_ids=true, to_apply=%region_26.32 | all-reduce | flops 256 | bytes 2048 | tf_op jit(solution)/shard_map/psum | solution.py:77
  831.1 125.2 %all-reduce.19.cloned.1.call-done = f32[64,1024]{1,0:T(8,128)} async-done(((f32[64,1024]{1,0:T(8,128)}), f32[64,1024]{1,0:T(8,128)}) %all-reduce.19.cloned.1.call-update) | async-done | bytes 262160 | tf_op jit(solution)/shard_map/psum | solution.py:53
  958.4 26.8 %psum.231 = f32[64,64]{0,1:T(8,128)S(1)} all-reduce(f32[64,64]{0,1:T(8,128)S(1)} %fusion.164), channel_id=1, replica_groups=mesh['smp'=8,'bld'=16] {'smp'}, use_global_device_ids=true, to_apply=%region_30.36 | all-reduce | flops 4096 | bytes 32768 | tf_op jit(solution)/shard_map/psum | solution.py:55
  1006.3 65.4 %all-reduce.21.cloned.1.call-done = f32[64,1024]{1,0:T(8,128)} async-done(((f32[64,1024]{1,0:T(8,128)}), f32[64,1024]{1,0:T(8,128)}) %all-reduce.21.cloned.1.call-update) | async-done | bytes 262160 | tf_op jit(solution)/shard_map/psum | solution.py:64
  1073.8 64.7 %psum.233 = f32[64,64]{0,1:T(8,128)S(1)} all-reduce(f32[64,64]{0,1:T(8,128)S(1)} %fusion.165), channel_id=1, replica_groups=mesh['smp'=8,'bld'=16] {'bld'}, use_global_device_ids=true, to_apply=%region_34.40 | all-reduce | flops 4096 | bytes 32768 | tf_op jit(solution)/shard_map/psum | solution.py:66
  1173.6 42.1 %psum.235 = f32[64,4]{0,1:T(4,128)S(1)} all-reduce(f32[64,4]{0,1:T(4,128)S(1)} %bitcast.372), channel_id=1, replica_groups=mesh['smp'=8,'bld'=16] {'bld'}, use_global_device_ids=true, to_apply=%region_38.44 | all-reduce | flops 256 | bytes 2048 | tf_op jit(solution)/shard_map/psum | solution.py:77
  1231.7 124.7 %all-reduce.23.cloned.1.call-done = f32[64,1024]{1,0:T(8,128)} async-done(((f32[64,1024]{1,0:T(8,128)}), f32[64,1024]{1,0:T(8,128)}) %all-reduce.23.cloned.1.call-update) | async-done | bytes 262160 | tf_op jit(solution)/shard_map/psum | solution.py:53
  1405.8 65.8 %all-reduce.25.cloned.1.call-done = f32[64,1024]{1,0:T(8,128)} async-done(((f32[64,1024]{1,0:T(8,128)}), f32[64,1024]{1,0:T(8,128)}) %all-reduce.25.cloned.1.call-update) | async-done | bytes 262160 | tf_op jit(solution)/shard_map/psum | solution.py:64
  1473.7 64.7 %psum.239 = f32[64,64]{0,1:T(8,128)S(1)} all-reduce(f32[64,64]{0,1:T(8,128)S(1)} %fusion.167), channel_id=1, replica_groups=mesh['smp'=8,'bld'=16] {'bld'}, use_global_device_ids=true, to_apply=%region_46.52 | all-reduce | flops 4096 | bytes 32768 | tf_op jit(solution)/shard_map/psum | solution.py:66
  1573.5 42.4 %psum.241 = f32[64,4]{0,1:T(4,128)S(1)} all-reduce(f32[64,4]{0,1:T(4,128)S(1)} %bitcast.373), channel_id=1, replica_groups=mesh['smp'=8,'bld'=16] {'bld'}, use_global_device_ids=true, to_apply=%region_50.56 | all-reduce | flops 256 | bytes 2048 | tf_op jit(solution)/shard_map/psum | solution.py:77
  1631.6 125.2 %all-reduce.27.cloned.1.call-done = f32[64,1024]{1,0:T(8,128)} async-done(((f32[64,1024]{1,0:T(8,128)}), f32[64,1024]{1,0:T(8,128)}) %all-reduce.27.cloned.1.call-update) | async-done | bytes 262160 | tf_op jit(solution)/shard_map/psum | solution.py:53
  1806.9 65.2 %all-reduce.29.cloned.1.call-done = f32[64,1024]{1,0:T(8,128)} async-done(((f32[64,1024]{1,0:T(8,128)}), f32[64,1024]{1,0:T(8,128)}) %all-reduce.29.cloned.1.call-update) | async-done | bytes 262160 | tf_op jit(solution)/shard_map/psum | solution.py:64
  1874.2 65.0 %psum.245 = f32[64,64]{0,1:T(8,128)S(1)} all-reduce(f32[64,64]{0,1:T(8,128)S(1)} %fusion.169), channel_id=1, replica_groups=mesh['smp'=8,'bld'=16] {'bld'}, use_global_device_ids=true, to_apply=%region_58.64 | all-reduce | flops 4096 | bytes 32768 | tf_op jit(solution)/shard_map/psum | solution.py:66
  1974.4 42.1 %psum.247 = f32[64,4]{0,1:T(4,128)S(1)} all-reduce(f32[64,4]{0,1:T(4,128)S(1)} %bitcast.374), channel_id=1, replica_groups=mesh['smp'=8,'bld'=16] {'bld'}, use_global_device_ids=true, to_apply=%region_62.68 | all-reduce | flops 256 | bytes 2048 | tf_op jit(solution)/shard_map/psum | solution.py:77
  (282 shorter events, 431.9 us)
Async XLA Ops:
  7.2 73.3 %copy-start.1 = (f32[4,64]{1,0:T(4,128)S(1)}, f32[4,64]{1,0:T(4,128)}, u32[]{:S(2)}) copy-start(f32[4,64]{1,0:T(4,128)} %param.14) | copy-start | bytes 3076
  7.2 7.6 copy-start
  7.2 148.4 %all-reduce.11.cloned.1.call-start = ((), (), s32[]{:S(2)}) async-start(), calls=%async_computation | async-start | bytes 524288 | tf_op jit(solution)/shard_map/psum | solution.py:53
  14.7 256.2 %all-reduce.13.cloned.1.call-start = ((), (), s32[]{:S(2)}) async-start(), calls=%async_computation.1 | async-start | bytes 524288 | tf_op jit(solution)/shard_map/psum | solution.py:64
  199.4 356.7 %all-reduce.15.cloned.1.call-start = ((), (), s32[]{:S(2)}) async-start(), calls=%async_computation.2 | async-start | bytes 524288 | tf_op jit(solution)/shard_map/psum | solution.py:53
  424.7 246.6 %all-reduce.17.cloned.1.call-start = ((), (), s32[]{:S(2)}) async-start(), calls=%async_computation.3 | async-start | bytes 524288 | tf_op jit(solution)/shard_map/psum | solution.py:64
  600.1 356.1 %all-reduce.19.cloned.1.call-start = ((), (), s32[]{:S(2)}) async-start(), calls=%async_computation.4 | async-start | bytes 524288 | tf_op jit(solution)/shard_map/psum | solution.py:53
  824.8 246.9 %all-reduce.21.cloned.1.call-start = ((), (), s32[]{:S(2)}) async-start(), calls=%async_computation.5 | async-start | bytes 524288 | tf_op jit(solution)/shard_map/psum | solution.py:64
  1000.6 355.8 %all-reduce.23.cloned.1.call-start = ((), (), s32[]{:S(2)}) async-start(), calls=%async_computation.6 | async-start | bytes 524288 | tf_op jit(solution)/shard_map/psum | solution.py:53
  1225.3 246.4 %all-reduce.25.cloned.1.call-start = ((), (), s32[]{:S(2)}) async-start(), calls=%async_computation.7 | async-start | bytes 524288 | tf_op jit(solution)/shard_map/psum | solution.py:64
  1400.1 356.7 %all-reduce.27.cloned.1.call-start = ((), (), s32[]{:S(2)}) async-start(), calls=%async_computation.8 | async-start | bytes 524288 | tf_op jit(solution)/shard_map/psum | solution.py:53
  1625.4 246.7 %all-reduce.29.cloned.1.call-start = ((), (), s32[]{:S(2)}) async-start(), calls=%async_computation.9 | async-start | bytes 524288 | tf_op jit(solution)/shard_map/psum | solution.py:64
Sparse Core Ops, SparseCore 0:
  14.8 140.7 all-reduce.10
  199.5 71.3 all-reduce.12
  424.8 131.2 all-reduce.14
  600.2 70.9 all-reduce.16
  825.0 131.2 all-reduce.18
  1000.7 70.9 all-reduce.20
  1225.4 130.9 all-reduce.22
  1400.2 71.3 all-reduce.24
  1625.5 131.2 all-reduce.26
  1800.7 71.3 all-reduce.28
